TPU v7x, 32 devices: a whole 2x2x4 slice. The times are simulated.
32 devices in a mesh: row: 8 (over z, y), col: 4 (over x, core).
Axes of the slice: x: 2, y: 2, z: 4, core: 2. Of those that a mesh axis runs over, the one named last changes fastest.
Arguments:
- env: float32 [512, 32768], P('row', 'col'), may hold values from -0.03125 to 0.03125
- wave: float32 [32768, 512], P('row', 'col'), may hold values from -6 to 6
- mpo: float32 [16, 16], replicated, may hold values from -1.5 to 1.5
Outputs:
- applied: float32 [512, 512], P('row', 'col')
All inputs are finite; a program needn't handle non-finite values.
Results may differ from a plain program's by a relative error of at most 0.00007.
Values sent between devices are 32-bit elements; how exact they have to be, the bound alone decides.
No kernel may reach another device: no remote copies, remote signals or barrier semaphores. Data moves between devices by JAX's collectives and lax.ppermute only.
A program may use at most 128 MiB of HBM per device.

v0:
```python
import jax
import jax.numpy as jnp
from jax import lax
from jax.sharding import PartitionSpec as P


def shards(env, wave, mpo):
    spins = mpo.shape[0]
    env_full = lax.all_gather(env, "col", axis=1, tiled=True)
    right_local = wave.shape[1] // spins
    partial_out = jnp.dot(
        env_full,
        lax.all_gather(wave, "row", axis=0, tiled=True),
        precision=lax.Precision.HIGHEST,
        preferred_element_type=jnp.float32,
    )
    out3 = partial_out.reshape(env.shape[0], right_local, spins)
    mixed = jnp.einsum("irs,st->itr", out3, mpo, precision=lax.Precision.HIGHEST)
    spun = lax.all_to_all(mixed, "col", split_axis=1, concat_axis=2, tiled=True)
    return spun.reshape(env.shape[0], -1)


def solution(mesh):
    in_specs = (P("row", "col"), P("row", "col"), P())
    out_specs = P("row", "col")
    return jax.shard_map(shards, mesh=mesh, in_specs=in_specs, out_specs=out_specs, check_vma=False)
```

profile of v0, /device:TPU:0, one launch (start us, length us, event | category | flops | bytes accessed | tf_op | source)
XLA Modules:
  0.0 345.3 jit_solution(17700859789182060455)
XLA Ops:
  6.5 0.0 copy-start
  6.5 0.0 all-gather.3.cloned.1.call-start
  6.5 0.7 all-gather.3.cloned.1.call-update
  7.3 0.0 all-gather.5.cloned.1.call-start
  7.3 0.7 all-gather.5.cloned.1.call-update
  8.0 61.9 %all-gather.3.cloned.1.call-done = f32[64,32768]{1,0:T(8,128)} async-done(((f32[64,8192]{1,0:T(8,128)}), f32[64,32768]{1,0:T(8,128)}) %all-gather.3.cloned.1.call-update) | async-done | bytes 8388624 | tf_op jit(solution)/shard_map/all_gather | solution.py:9
  69.9 229.4 %all-gather.5.cloned.1.call-done = f32[32768,128]{1,0:T(8,128)} async-done(((f32[4096,128]{1,0:T(8,128)}), f32[32768,128]{1,0:T(8,128)}) %all-gather.5.cloned.1.call-update) | async-done | bytes 16777232 | tf_op jit(solution)/shard_map/all_gather | solution.py:13
  299.4 30.2 %fusion.1 = f32[64,128]{0,1:T(8,128)S(1)} fusion(f32[64,32768]{1,0:T(8,128)} %all-gather.3.cloned.1.call-done, f32[32768,128]{1,0:T(8,128)} %all-gather.5.cloned.1.call-done), kind=kOutput, calls=%fused_computation.3 | convolution fusion | flops 3221225472 | bytes 25198592 | tf_op jit(solution)/shard_map/dot_general | solution.py:11
  329.5 0.0 copy-done
  329.5 0.3 convolution_bitcast_fusion
  329.8 0.1 reshape.10
  329.9 6.5 %all_to_all.15 = f32[4,1,2048]{2,1,0:T(1,128)S(1)} all-to-all(f32[4,1,2048]{2,1,0:T(1,128)S(1)} %reshape.10), channel_id=1, replica_groups=mesh['row'=8,'col'=4] {'col'}, dimensions={0} | all-to-all | bytes 65536 | tf_op jit(solution)/shard_map/all_to_all | solution.py:19
  336.4 0.5 broadcast
  336.9 0.7 reduce
  337.7 0.1 reshape.11
  337.8 0.7 copy.15
  (2 shorter events, 0.0 us)
Async XLA Ops:
  6.5 323.0 %copy-start = (f32[16,16]{1,0:T(8,128)S(1)}, f32[16,16]{1,0:T(8,128)}, u32[]{:S(2)}) copy-start(f32[16,16]{1,0:T(8,128)} %param.5) | copy-start | bytes 3076
  6.5 63.4 %all-gather.3.cloned.1.call-start = ((), (), s32[]{:S(2)}) async-start(), calls=%async_computation.1 | async-start | bytes 10485760 | tf_op jit(solution)/shard_map/all_gather | solution.py:9
  7.3 292.1 %all-gather.5.cloned.1.call-start = ((), (), s32[]{:S(2)}) async-start(), calls=%async_computation.2 | async-start | bytes 18874368 | tf_op jit(solution)/shard_map/all_gather | solution.py:13
Sparse Core Ops, SparseCore 0:
  8.9 60.9 all-gather.2
  72.0 227.2 all-gather.4
where the time goes:
time: 345 us
  waiting for transfers between devices  293 us (85%)
  matrix products  30.4 us (9%)
  between operations  13.4 us (4%)
  blocking collectives  6.49 us (2%)
    all_gather x1, waiting for transfers between devices, shards(): lax.all_gather(wave, 'row', axis=0, tiled=True)  229 us
    all_gather x1, waiting for transfers between devices, shards(): env_full = lax.all_gather(env, 'col', axis=1, tiled=True)  61.9 us
    dot_general x1, matrix products, shards(): jnp.dot(env_full, lax.all_gather(wave, 'row', axis=0, tiled=True), precis...  30.2 us
  transfers between devices with their start and end apart: 2, of which 2 were waited for; matrix products, arithmetic and copies ran while one was open for 0% of the time, Pallas kernels for 0%

commit v1 on v0

--- a/solution.py
+++ b/solution.py
@@ -4,9 +4,19 @@
 from jax.sharding import PartitionSpec as P
 
 
+def pass_along(array, mesh_axis, along):
+    size = lax.axis_size(mesh_axis)
+    moving, blocks = (array, [array])
+    for _ in range(size - 1):
+        moving = lax.ppermute(moving, mesh_axis, [(i, (i + 1) % size) for i in range(size)])
+        blocks.insert(0, moving)
+    line = jnp.concatenate(blocks, axis=along)
+    return jnp.roll(line, (lax.axis_index(mesh_axis) + 1) * array.shape[along], axis=along)
+
+
 def shards(env, wave, mpo):
     spins = mpo.shape[0]
-    env_full = lax.all_gather(env, "col", axis=1, tiled=True)
+    env_full = pass_along(env, "col", 1)
     right_local = wave.shape[1] // spins
     partial_out = jnp.dot(
         env_full,

time: 345 us -> 286 us (0.83)
  waiting for transfers between devices: 293 us -> 209 us
  local copies, waits for them, and re-layouts: 1.44 us -> 24.6 us
    all_gather x1, waiting for transfers between devices: 229 us -> 131 us  [shards(): lax.all_gather(wave, 'row', axis=0, tiled=True)]
    ppermute x0 -> x3, waiting for transfers between devices: none -> 77.1 us  [pass_along(): lax.ppermute(moving, mesh_axis, [(i, (i + 1) % size) for i in range(size)])]
    all_gather x1 -> x0, waiting for transfers between devices: 61.9 us -> none  [shards(): env_full = lax.all_gather(env, 'col', axis=1, tiled=True)]
    unnamed x4 -> x17, local copies, waits for them, and re-layouts: 0.2 us -> 22 us
  transfers between devices with their start and end apart: 2 -> 4, of which waited for: 2 -> 4; matrix products, arithmetic and copies ran while one was open for 0% -> 8% of each run, Pallas kernels for 0% -> 0%
where the time goes in v1:
time: 286 us; the launch traced here: 285 us
  waiting for transfers between devices  209 us (73%)
  matrix products  30.4 us (11%)
  local copies, waits for them, and re-layouts  24.6 us (9%)
  between operations  13.4 us (5%)
  blocking collectives  6.48 us (2%)
    all_gather x1, waiting for transfers between devices, shards(): lax.all_gather(wave, 'row', axis=0, tiled=True)  131 us
    ppermute x3, waiting for transfers between devices, pass_along(): lax.ppermute(moving, mesh_axis, [(i, (i + 1) % size) for i in range(size)])  77.1 us
    dot_general x1, matrix products, shards(): jnp.dot(env_full, lax.all_gather(wave, 'row', axis=0, tiled=True), precis...  30.2 us
    unnamed x17, local copies, waits for them, and re-layouts  22 us
    all_to_all x1, blocking collectives, shards(): spun = lax.all_to_all(mixed, 'col', split_axis=1, concat_axis=2, tiled=True)  6.48 us
  transfers between devices with their start and end apart: 4, of which 4 were waited for; matrix products, arithmetic and copies ran while one was open for 8% of the time, Pallas kernels for 0%

profile of v1, /device:TPU:0, one launch (start us, length us, event | category | flops | bytes accessed | tf_op | source)
XLA Modules:
  0.0 285.5 jit_solution(1375108238469908680)
XLA Ops:
  6.5 0.7 all-gather.2.cloned.1.call-update
  7.3 0.5 collective-permute-start
  7.8 25.8 %collective-permute-done = f32[64,8192]{1,0:T(8,128)S(1)} collective-permute-done((f32[64,8192]{1,0:T(8,128)}, f32[64,8192]{1,0:T(8,128)S(1)}, u32[]{:S(2)}, u32[]{:S(2)}) %collective-permute-start) | collective-permute-done | bytes 2097184 | tf_op jit(solution)/shard_map/ppermute | solution.py:11
  33.7 1.3 copy-done.2
  35.0 0.0 collective-permute-start.1
  35.0 25.5 %collective-permute-done.1 = f32[64,8192]{1,0:T(8,128)} collective-permute-done((f32[64,8192]{1,0:T(8,128)S(1)}, f32[64,8192]{1,0:T(8,128)}, u32[]{:S(2)}, u32[]{:S(2)}) %collective-permute-start.1) | collective-permute-done | bytes 2097184 | tf_op jit(solution)/shard_map/ppermute | solution.py:11
  60.6 25.8 %collective-permute-done.2 = f32[64,8192]{1,0:T(8,128)} collective-permute-done((f32[64,8192]{1,0:T(8,128)}, f32[64,8192]{1,0:T(8,128)}, u32[]{:S(2)}, u32[]{:S(2)}) %collective-permute-start.2) | collective-permute-done | bytes 2097184 | tf_op jit(solution)/shard_map/ppermute | solution.py:11
  86.3 3.0 %constant_dynamic-update-slice_fusion.7 = f32[64,65536]{1,0:T(8,128)} fusion(f32[64,8192]{1,0:T(8,128)} %collective-permute-done.2), kind=kLoop, calls=%fused_computation.10 | loop fusion | bytes 4194304
  89.4 3.0 %constant_dynamic-update-slice_fusion.6 = f32[64,65536]{1,0:T(8,128)} fusion(f32[64,65536]{1,0:T(8,128)} %constant_dynamic-update-slice_fusion.7, f32[64,8192]{1,0:T(8,128)} %collective-permute-done.1), kind=kLoop, calls=%fused_computation.9 | loop fusion | bytes 4194304
  92.4 3.0 %constant_dynamic-update-slice_fusion.5 = f32[64,65536]{1,0:T(8,128)} fusion(f32[64,65536]{1,0:T(8,128)} %constant_dynamic-update-slice_fusion.6, f32[64,8192]{1,0:T(8,128)} %copy-done.2), kind=kLoop, calls=%fused_computation.8 | loop fusion | bytes 4194304
  95.4 3.1 %constant_dynamic-update-slice_fusion.4 = f32[64,65536]{1,0:T(8,128)} fusion(f32[64,65536]{1,0:T(8,128)} %constant_dynamic-update-slice_fusion.5, f32[64,8192]{1,0:T(8,128)} %param.3), kind=kLoop, calls=%fused_computation.7 | loop fusion | bytes 4194304
  98.5 3.6 %constant_dynamic-update-slice_fusion.3 = f32[64,65536]{1,0:T(8,128)} fusion(f32[64,65536]{1,0:T(8,128)} %constant_dynamic-update-slice_fusion.4, f32[64,8192]{1,0:T(8,128)} %collective-permute-done.2), kind=kLoop, calls=%fused_computation.6 | loop fusion | bytes 4194304
  102.1 3.2 %constant_dynamic-update-slice_fusion.2 = f32[64,65536]{1,0:T(8,128)} fusion(f32[64,65536]{1,0:T(8,128)} %constant_dynamic-update-slice_fusion.3, f32[64,8192]{1,0:T(8,128)} %collective-permute-done.1), kind=kLoop, calls=%fused_computation.5 | loop fusion | bytes 4194304
  105.4 1.4 constant_dynamic-update-slice_fusion.1
  106.8 1.4 constant_dynamic-update-slice_fusion
  108.2 131.3 %all-gather.2.cloned.1.call-done = f32[32768,128]{1,0:T(8,128)} async-done(((f32[4096,128]{1,0:T(8,128)}), f32[32768,128]{1,0:T(8,128)}) %all-gather.2.cloned.1.call-update) | async-done | bytes 16777232 | tf_op jit(solution)/shard_map/all_gather | solution.py:23
  239.5 30.2 %fusion = f32[64,128]{0,1:T(8,128)S(1)} fusion(f32[32768,128]{1,0:T(8,128)} %all-gather.2.cloned.1.call-done, f32[64,65536]{1,0:T(8,128)} %constant_dynamic-update-slice_fusion, s32[]{:T(128)S(6)} %select_n.14), kind=kOutput, calls=%fused_computation | convolution fusion | flops 3221225472 | bytes 25198596 | tf_op jit(solution)/shard_map/dot_general | solution.py:21
  269.7 0.3 convolution_bitcast_fusion
  270.0 0.1 reshape.10
  270.1 6.5 %all_to_all.15 = f32[4,1,2048]{2,1,0:T(1,128)S(1)} all-to-all(f32[4,1,2048]{2,1,0:T(1,128)S(1)} %reshape.10), channel_id=1, replica_groups=mesh['row'=8,'col'=4] {'col'}, dimensions={0} | all-to-all | bytes 65536 | tf_op jit(solution)/shard_map/all_to_all | solution.py:29
  276.6 0.5 broadcast.1
  277.1 0.7 reduce
  277.8 0.1 reshape.11
  277.9 0.7 copy.15
  (11 shorter events, 0.0 us)
Async XLA Ops:
  6.5 263.1 %copy-start = (f32[16,16]{1,0:T(8,128)S(1)}, f32[16,16]{1,0:T(8,128)}, u32[]{:S(2)}) copy-start(f32[16,16]{1,0:T(8,128)} %param.5) | copy-start | bytes 3076
  6.5 100.2 %copy-start.1 = (f32[64,8192]{1,0:T(8,128)S(1)}, f32[64,8192]{1,0:T(8,128)}, u32[]{:S(2)}) copy-start(f32[64,8192]{1,0:T(8,128)} %param.3) | copy-start | bytes 6291460
  6.5 233.0 %all-gather.2.cloned.1.call-start = ((), (), s32[]{:S(2)}) async-start(), calls=%async_computation.1 | async-start | bytes 18874368 | tf_op jit(solution)/shard_map/all_gather | solution.py:23
  7.3 26.4 %collective-permute-start = (f32[64,8192]{1,0:T(8,128)}, f32[64,8192]{1,0:T(8,128)S(1)}, u32[]{:S(2)}, u32[]{:S(2)}) collective-permute-start(f32[64,8192]{1,0:T(8,128)} %param.3), channel_id=1, source_target_pairs={{0,1},{1,2},{2,3},{3,0},{4,5},{5,6},{6,7},{7,4},{8,9},{9,10},{10,1... | collective-permute-start | bytes 6291464 | tf_op jit(solution)/shard_map/ppermute | solution.py:11
  33.7 1.3 copy-start.2
  35.0 25.6 %collective-permute-start.1 = (f32[64,8192]{1,0:T(8,128)S(1)}, f32[64,8192]{1,0:T(8,128)}, u32[]{:S(2)}, u32[]{:S(2)}) collective-permute-start(f32[64,8192]{1,0:T(8,128)S(1)} %collective-permute-done), channel_id=1, source_target_pairs={{0,1},{1,2},{2,3},{3,0},{4,5},{5,6},{6,7},{7,4},{8,9},{9,10},{10,1... | collective-permute-start | bytes 6291464 | tf_op jit(solution)/shard_map/ppermute | solution.py:11
  60.6 25.8 %collective-permute-start.2 = (f32[64,8192]{1,0:T(8,128)}, f32[64,8192]{1,0:T(8,128)}, u32[]{:S(2)}, u32[]{:S(2)}) collective-permute-start(f32[64,8192]{1,0:T(8,128)} %collective-permute-done.1), channel_id=1, source_target_pairs={{0,1},{1,2},{2,3},{3,0},{4,5},{5,6},{6,7},{7,4},{8,9},{9,10},{10,1... | collective-permute-start | bytes 6291464 | tf_op jit(solution)/shard_map/ppermute | solution.py:11
  60.6 44.8 %copy-start.3 = (f32[64,8192]{1,0:T(8,128)S(1)}, f32[64,8192]{1,0:T(8,128)}, u32[]{:S(2)}) copy-start(f32[64,8192]{1,0:T(8,128)} %copy-done.2) | copy-start | bytes 6291460
Sparse Core Ops, SparseCore 0:
  9.5 229.9 all-gather.1
